TPU v7x, 32 devices: a whole 2x2x4 slice. The times are simulated.
32 devices in a mesh: dp: 8 (over y, x, core), tensor: 4 (over z).
Axes of the slice: x: 2, y: 2, z: 4, core: 2. Of those that a mesh axis runs over, the one named last changes fastest.
Arguments:
- x_in: bfloat16 [16384, 768], P(('dp', 'tensor')), may hold values from -6 to 6
- bucket: int32 [32], P(('dp', 'tensor')), may hold values from 0 to 1
- lengths: int32 [32, 4], P(('dp', 'tensor')), may hold values from 32 to 128, as said below
- qkv_weight: bfloat16 [2, 768, 2304], replicated, may hold values from -0.21875 to 0.21875
- out_weight: bfloat16 [2, 768, 768], replicated, may hold values from -0.875 to 0.875
- norm_gain1: float32 [2, 768], replicated, may hold values from 0.5 to 1.5
- norm_bias1: float32 [2, 768], replicated, may hold values from -1.8 to 1.8
- up_weight: bfloat16 [2, 768, 2, 3072], P(None, None, None, 'tensor'), may hold values from -0.21875 to 0.21875
- down_weight: bfloat16 [2, 3072, 768], P(None, 'tensor'), may hold values from -0.109375 to 0.109375
- norm_gain2: float32 [2, 768], replicated, may hold values from 0.5 to 1.5
- norm_bias2: float32 [2, 768], replicated, may hold values from -1.8 to 1.8
- cotangent: bfloat16 [16384, 768], P(('dp', 'tensor')), may hold values from -6 to 6
Outputs:
- activations: bfloat16 [2, 16384, 768], P(None, ('dp', 'tensor'))
- input_grad: float32 [16384, 768], P(('dp', 'tensor'))
- qkv_grad: float32 [2, 768, 2304], replicated
- out_grad: float32 [2, 768, 768], replicated
- gain1_grad: float32 [2, 768], replicated
- bias1_grad: float32 [2, 768], replicated
- up_grad: float32 [2, 768, 2, 3072], P(None, 'dp', None, 'tensor')
- down_grad: float32 [2, 3072, 768], P(None, 'tensor', 'dp')
- gain2_grad: float32 [2, 768], replicated
- bias2_grad: float32 [2, 768], replicated
Inputs may be any that keep to these rules, and one draw needn't show every extreme that they name: Every entry is a length of a short sequence; each row of lengths has an entry equal to 128. A block of bucket 1 holds one sequence whose length is the sum of its row of lengths.
All inputs are finite; a program needn't handle non-finite values.
Results may differ from a plain program's by a relative error of at most 0.033.
Values may be sent and summed in bfloat16 or wider, within the bound.
No kernel may reach another device: no remote copies, remote signals or barrier semaphores. Data moves between devices by JAX's collectives and lax.ppermute only.
A program may use at most 256 MiB of HBM per device.

v0:
```python
import jax
import jax.numpy as jnp
from jax import lax
from jax.sharding import PartitionSpec as P

HEADS = 12
HEAD_DIM = 64
SHORT = 128
LAYERS = 2
eps_norm = 1e-05
gelu_coef = 0.7978845608028654
masked_score = -1e30


def segments(bucket_one, lens, rows_dev, short_len):
    rows = jnp.arange(rows_dev, dtype=jnp.int32)
    slot = rows // short_len
    offset = rows - slot * short_len
    slots_all = jnp.arange(lens.shape[0], dtype=jnp.int32)
    slot_len = jnp.sum(jnp.where(slot[:, None] == slots_all[None, :], lens[None, :], 0), axis=1)
    total = jnp.sum(lens)
    is_long = bucket_one == 1
    real = jnp.where(is_long, rows < total, offset < slot_len)
    group = jnp.where(is_long, 0, slot)
    return jnp.where(real, group, lens.shape[0] + rows)


def alibi(rows_dev, heads):
    slopes = jnp.exp2(-8.0 * (jnp.arange(heads, dtype=jnp.float32) + 1.0) / heads)
    place = jnp.arange(rows_dev, dtype=jnp.float32)
    dist = jnp.abs(place[:, None] - place[None, :])
    return slopes[:, None, None] * dist[None, :, :]


def layer_norm(value, gain, bias):
    mean = jnp.mean(value, axis=-1, keepdims=True)
    centered = value - mean
    var = jnp.mean(centered * centered, axis=-1, keepdims=True)
    return centered * lax.rsqrt(var + eps_norm) * gain + bias


def geglu(joined):
    half = joined.shape[1] // 2
    gate = joined[:, :half]
    value = joined[:, half:]
    return 0.5 * gate * (1.0 + jnp.tanh(gelu_coef * (gate + 0.044715 * gate * gate * gate))) * value


def split_heads(qkv_low, width):
    rows = qkv_low.shape[0]
    query = qkv_low[:, :width].reshape(rows, HEADS, HEAD_DIM)
    keys = qkv_low[:, width : 2 * width].reshape(rows, HEADS, HEAD_DIM)
    values = qkv_low[:, 2 * width :].reshape(rows, HEADS, HEAD_DIM)
    return (query, keys, values)


def scores_of(query, keys, same, decay):
    raw = (
        jnp.einsum("qhe,khe->hqk", query, keys, preferred_element_type=jnp.float32)
        * HEAD_DIM ** (-0.5)
        - decay
    )
    return jnp.where(same[None, :, :], raw, masked_score)


def forward_layer(x_low, wqkv, wo, g1, b1, wup, wdown, g2, b2, same, decay):
    rows = x_low.shape[0]
    width = x_low.shape[1]
    qkv_low = jnp.dot(x_low, wqkv, preferred_element_type=jnp.float32).astype(jnp.bfloat16)
    query, keys, values = split_heads(qkv_low, width)
    scores = scores_of(query, keys, same, decay)
    top = jnp.max(scores, axis=-1, keepdims=True)
    log_total = top + jnp.log(jnp.sum(jnp.exp(scores - top), axis=-1, keepdims=True))
    probs_low = jnp.exp(scores - log_total).astype(jnp.bfloat16)
    ctx_low = (
        jnp.einsum("hqk,khe->qhe", probs_low, values, preferred_element_type=jnp.float32)
        .reshape(rows, width)
        .astype(jnp.bfloat16)
    )
    attn = jnp.dot(ctx_low, wo, preferred_element_type=jnp.float32)
    pre_first = x_low.astype(jnp.float32) + attn
    normed = layer_norm(pre_first, g1, b1)
    normed_low = normed.astype(jnp.bfloat16)
    gathered = lax.all_gather(normed_low, "tensor", axis=0, tiled=True)
    joined = jnp.dot(gathered, wup.reshape(width, -1), preferred_element_type=jnp.float32)
    act_low = geglu(joined).astype(jnp.bfloat16)
    mixed = lax.psum_scatter(
        jnp.dot(act_low, wdown, preferred_element_type=jnp.float32).astype(jnp.bfloat16),
        "tensor",
        scatter_dimension=0,
        tiled=True,
    ).astype(jnp.float32)
    pre_second = normed + mixed
    out_low = layer_norm(pre_second, g2, b2).astype(jnp.bfloat16)
    keep = (
        x_low,
        qkv_low,
        log_total,
        ctx_low,
        pre_first,
        normed_low,
        pre_second,
        gathered,
        joined,
        act_low,
    )
    return (out_low, keep)


def backward_layer(grad_out, keep, wqkv, wo, g1, b1, wup, wdown, g2, b2, same, decay):
    (
        x_low,
        qkv_low,
        log_total,
        ctx_low,
        pre_first,
        normed_low,
        pre_second,
        gathered,
        joined,
        act_low,
    ) = keep
    rows = x_low.shape[0]
    width = x_low.shape[1]
    up_flat = wup.reshape(width, -1)
    second_pull = jax.vjp(layer_norm, pre_second, g2, b2)[1]
    d_pre2, d_gain2, d_bias2 = second_pull(grad_out)
    grad_rows = lax.all_gather(d_pre2.astype(jnp.bfloat16), "tensor", axis=0, tiled=True)
    d_act = jnp.dot(grad_rows, wdown.T, preferred_element_type=jnp.float32)
    d_down = jnp.dot(act_low.T, grad_rows, preferred_element_type=jnp.float32)
    geglu_pull = jax.vjp(geglu, joined)[1]
    d_joined = geglu_pull(d_act)[0].astype(jnp.bfloat16)
    d_up = jnp.dot(gathered.T, d_joined, preferred_element_type=jnp.float32).reshape(wup.shape)
    d_normed = d_pre2 + lax.psum_scatter(
        jnp.dot(d_joined, up_flat.T, preferred_element_type=jnp.float32).astype(jnp.bfloat16),
        "tensor",
        scatter_dimension=0,
        tiled=True,
    ).astype(jnp.float32)
    first_pull = jax.vjp(layer_norm, pre_first, g1, b1)[1]
    d_pre1, d_gain1, d_bias1 = first_pull(d_normed)
    d_attn_low = d_pre1.astype(jnp.bfloat16)
    d_wo = jnp.dot(ctx_low.T, d_attn_low, preferred_element_type=jnp.float32)
    d_ctx = (
        jnp.dot(d_attn_low, wo.T, preferred_element_type=jnp.float32)
        .astype(jnp.bfloat16)
        .reshape(rows, HEADS, HEAD_DIM)
    )
    query, keys, values = split_heads(qkv_low, width)
    probs = jnp.exp(scores_of(query, keys, same, decay) - log_total)
    probs_low = probs.astype(jnp.bfloat16)
    d_values = jnp.einsum("hqk,qhe->khe", probs_low, d_ctx, preferred_element_type=jnp.float32)
    d_probs = jnp.einsum("qhe,khe->hqk", d_ctx, values, preferred_element_type=jnp.float32)
    d_scores = (probs * (d_probs - jnp.sum(probs * d_probs, axis=-1, keepdims=True))).astype(
        jnp.bfloat16
    )
    d_query = jnp.einsum(
        "hqk,khe->qhe", d_scores, keys, preferred_element_type=jnp.float32
    ) * HEAD_DIM ** (-0.5)
    d_keys = jnp.einsum(
        "hqk,qhe->khe", d_scores, query, preferred_element_type=jnp.float32
    ) * HEAD_DIM ** (-0.5)
    d_qkv = jnp.concatenate(
        [d_query.reshape(rows, width), d_keys.reshape(rows, width), d_values.reshape(rows, width)],
        axis=1,
    ).astype(jnp.bfloat16)
    d_wqkv = jnp.dot(x_low.T, d_qkv, preferred_element_type=jnp.float32)
    d_input = d_pre1 + jnp.dot(d_qkv, wqkv.T, preferred_element_type=jnp.float32)
    return (d_input, d_wqkv, d_wo, d_gain1, d_bias1, d_up, d_down, d_gain2, d_bias2)


def shards(
    x_in,
    bucket,
    lengths,
    qkv_weight,
    out_weight,
    norm_gain1,
    norm_bias1,
    up_weight,
    down_weight,
    norm_gain2,
    norm_bias2,
    cotangent,
):
    rows = x_in.shape[0]
    seg = segments(bucket[0], lengths[0], rows, SHORT)
    same = seg[:, None] == seg[None, :]
    decay = alibi(rows, HEADS)
    layer_in = x_in
    outputs = []
    kept = []
    for layer in range(LAYERS):
        layer_in, keep = forward_layer(
            layer_in,
            qkv_weight[layer],
            out_weight[layer],
            norm_gain1[layer],
            norm_bias1[layer],
            up_weight[layer],
            down_weight[layer],
            norm_gain2[layer],
            norm_bias2[layer],
            same,
            decay,
        )
        outputs.append(layer_in)
        kept.append(keep)
    grad = cotangent.astype(jnp.float32)
    found = [None] * LAYERS
    for layer in reversed(range(LAYERS)):
        grad, d_wqkv, d_wo, d_gain1, d_bias1, d_up, d_down, d_gain2, d_bias2 = backward_layer(
            grad,
            kept[layer],
            qkv_weight[layer],
            out_weight[layer],
            norm_gain1[layer],
            norm_bias1[layer],
            up_weight[layer],
            down_weight[layer],
            norm_gain2[layer],
            norm_bias2[layer],
            same,
            decay,
        )
        d_wqkv, d_wo, d_gain1, d_bias1, d_gain2, d_bias2 = lax.psum(
            (d_wqkv, d_wo, d_gain1, d_bias1, d_gain2, d_bias2), ("dp", "tensor")
        )
        d_up, d_down = (
            lax.psum_scatter(
                d_up.astype(jnp.bfloat16), "dp", scatter_dimension=0, tiled=True
            ).astype(jnp.float32),
            lax.psum_scatter(
                d_down.astype(jnp.bfloat16), "dp", scatter_dimension=1, tiled=True
            ).astype(jnp.float32),
        )
        found[layer] = (d_wqkv, d_wo, d_gain1, d_bias1, d_up, d_down, d_gain2, d_bias2)
    stacked = [jnp.stack([found[layer][index] for layer in range(LAYERS)]) for index in range(8)]
    qkv_grad, out_grad, gain1_grad, bias1_grad, up_grad, down_grad, gain2_grad, bias2_grad = stacked
    activations = jnp.stack(outputs)
    return (
        activations,
        grad,
        qkv_grad,
        out_grad,
        gain1_grad,
        bias1_grad,
        up_grad,
        down_grad,
        gain2_grad,
        bias2_grad,
    )


def solution(mesh):
    in_specs = (
        P(("dp", "tensor"), None),
        P(("dp", "tensor")),
        P(("dp", "tensor"), None),
        P(),
        P(),
        P(),
        P(),
        P(None, None, None, "tensor"),
        P(None, "tensor", None),
        P(),
        P(),
        P(("dp", "tensor"), None),
    )
    out_specs = (
        P(None, ("dp", "tensor"), None),
        P(("dp", "tensor"), None),
        P(),
        P(),
        P(),
        P(),
        P(None, "dp", None, "tensor"),
        P(None, "tensor", "dp"),
        P(),
        P(),
    )
    return jax.shard_map(shards, mesh=mesh, in_specs=in_specs, out_specs=out_specs, check_vma=False)
```

profile of v0, /device:TPU:0, one launch (start us, length us, event | category | flops | bytes accessed | tf_op | source)
XLA Modules:
  0.0 1206.9 jit_solution(10613801410674038543)
XLA Ops:
  12.0 4.2 convolution_convert_fusion.1
  17.3 5.0 fusion.103
  24.3 2.6 copy-done
  26.9 2.1 fusion.42
  32.5 7.0 fusion.100
  39.5 1.9 copy.111
  41.4 57.2 %all-gather.5.cloned.1.call-done = bf16[2048,768]{1,0:T(8,128)(2,1)} async-done(((bf16[512,768]{1,0:T(8,128)(2,1)}), bf16[2048,768]{1,0:T(8,128)(2,1)}) %all-gather.5.cloned.1.call-update) | async-done | bytes 3145744 | tf_op jit(solution)/shard_map/all_gather | solution.py:84
  98.6 7.7 fusion.107
  106.4 2.2 multiply_convert_fusion.3
  108.6 2.8 copy-done.8
  113.1 3.9 convolution_convert_fusion.5
  117.8 58.3 %reduce-scatter.7.cloned.1.call-done = bf16[512,768]{1,0:T(8,128)(2,1)} async-done(((bf16[2048,768]{1,0:T(8,128)(2,1)}), bf16[512,768]{1,0:T(8,128)(2,1)}) %reduce-scatter.7.cloned.1.call-update) | async-done | bytes 786448 | tf_op jit(solution)/shard_map/reduce_scatter | solution.py:87
  178.1 4.1 convolution_convert_fusion
  187.6 4.9 fusion.105
  194.4 2.6 copy-done.1
  197.0 2.1 fusion.48
  201.9 3.5 copy.112
  205.4 60.0 %all-gather.7.cloned.1.call-done = bf16[2048,768]{1,0:T(8,128)(2,1)} async-done(((bf16[512,768]{1,0:T(8,128)(2,1)}), bf16[2048,768]{1,0:T(8,128)(2,1)}) %all-gather.7.cloned.1.call-update) | async-done | bytes 3145744 | tf_op jit(solution)/shard_map/all_gather | solution.py:84
  265.3 7.7 fusion.108
  273.1 2.2 multiply_convert_fusion.2
  275.3 2.8 copy-done.9
  279.7 3.9 convolution_convert_fusion.4
  283.7 59.0 %reduce-scatter.9.cloned.1.call-done = bf16[512,768]{1,0:T(8,128)(2,1)} async-done(((bf16[2048,768]{1,0:T(8,128)(2,1)}), bf16[512,768]{1,0:T(8,128)(2,1)}) %reduce-scatter.9.cloned.1.call-update) | async-done | bytes 786448 | tf_op jit(solution)/shard_map/reduce_scatter | solution.py:87
  350.1 63.4 %all-gather.9.cloned.1.call-done = bf16[2048,768]{1,0:T(8,128)(2,1)} async-done(((bf16[512,768]{1,0:T(8,128)(2,1)}), bf16[2048,768]{1,0:T(8,128)(2,1)}) %all-gather.9.cloned.1.call-update) | async-done | bytes 3145744 | tf_op jit(solution)/shard_map/all_gather | solution.py:128
  413.6 12.0 fusion.25
  425.6 2.6 copy-done.79
  428.2 2.0 copy-done.80
  430.2 6.4 convolution_convert_fusion.7
  436.7 59.0 %reduce-scatter.11.cloned.1.call-done = bf16[512,768]{1,0:T(8,128)(2,1)} async-done(((bf16[2048,768]{1,0:T(8,128)(2,1)}), bf16[512,768]{1,0:T(8,128)(2,1)}) %reduce-scatter.11.cloned.1.call-update) | async-done | bytes 786448 | tf_op jit(solution)/shard_map/reduce_scatter | solution.py:134
  495.7 3.2 multiply_reduce_fusion.3
  502.1 7.7 fusion.51
  509.8 9.2 multiply_reduce_fusion.1
  519.0 6.9 multiply_convert_fusion.1
  526.0 2.0 multiply_convert_fusion.6
  531.2 2.6 multiply_reduce_fusion.2
  536.6 63.6 %all-gather.11.cloned.1.call-done = bf16[2048,768]{1,0:T(8,128)(2,1)} async-done(((bf16[512,768]{1,0:T(8,128)(2,1)}), bf16[2048,768]{1,0:T(8,128)(2,1)}) %all-gather.11.cloned.1.call-update) | async-done | bytes 3145744 | tf_op jit(solution)/shard_map/all_gather | solution.py:128
  600.3 12.6 %fusion.24 = (f32[2048,768]{1,0:T(8,128)S(1)}, f32[2048,768]{1,0:T(8,128)S(1)}) fusion(f32[2048,1536]{1,0:T(8,128)} %copy-done.8, bf16[2048,768]{1,0:T(8,128)(2,1)} %all-gather.11.cloned.1.call-done, bf16[2,768,768]{2,1,0:T(8,128)(2,1)} %param.20), kind=kOutput, calls=%fused_computation.69 | convolution fusion | flops 2456813568 | bytes 29491200 | tf_op jit(solution)/shard_map/dot_general | solution.py:129
  612.8 2.7 copy-done.81
  615.5 2.1 copy-done.82
  617.6 6.4 convolution_convert_fusion.6
  624.1 6.5 convolution_convert_fusion.8
  630.9 12.0 convolution_convert_fusion.2
  642.9 6.0 convert_element_type.181
  648.9 6.6 convolution_convert_fusion.9
  655.8 3.6 convolution_bitcast_fusion.2
  659.4 5.0 convolution_bitcast_fusion
  664.5 9.3 convolution_convert_fusion.3
  673.7 6.0 convert_element_type.179
  679.8 3.3 reduce-scatter.13.cloned.1.call-done
  683.1 2.6 multiply_reduce_fusion.4
  691.0 10.9 multiply_reduce_fusion
  704.0 7.0 multiply_convert_fusion
  711.1 2.3 convolution_bitcast_fusion.3
  713.4 2.0 multiply_convert_fusion.4
  716.6 2.0 fusion.45
  719.5 5.0 convolution_bitcast_fusion.1
  728.1 35.8 %reduce-scatter.15.cloned.1.call-done = bf16[768,96]{0,1:T(8,128)(2,1)} async-done(((bf16[768,768]{0,1:T(8,128)(2,1)}), bf16[768,96]{0,1:T(8,128)(2,1)}) %reduce-scatter.15.cloned.1.call-update) | async-done | bytes 147472 | tf_op jit(solution)/shard_map/reduce_scatter | solution.py:233
  765.8 88.5 %all-reduce.14.cloned.1.call-done = (bf16[768,2,768]{2,1,0:T(2,128)(2,1)}, bf16[768,2,768]{2,1,0:T(2,128)(2,1)}) async-done(((bf16[768,2,768]{2,1,0:T(2,128)(2,1)}, bf16[768,2,768]{2,1,0:T(2,128)(2,1)}), (bf16[768,2,768]{2,1,0:T(2,128)(2,1)}, bf16[768,2,768]{2,1,0:T(2,128)(2,1)})) %all-reduce.14.cloned.1.call-update) | async-done | bytes 4718608
  858.5 41.8 %all-reduce.6 = (f32[1,768]{1,0:T(1,128)S(1)}, f32[1,768]{1,0:T(1,128)S(1)}, f32[1,768]{1,0:T(1,128)S(1)}, f32[1,768]{1,0:T(1,128)S(1)}, f32[1,768]{1,0:T(1,128)...) all-reduce(f32[1,768]{1,0:T(1,128)S(1)} %stack.101, ...), channel_id=1, replica_groups=mesh['dp'=8,'tensor'=4] {'dp','tensor'}, use_global_device_ids=true, to_apply=%region_35.36 | all-reduce | flops 6144 | bytes 49152 | tf_op jit(solution)/shard_map/psum | solution.py:226
  902.7 5.5 add_add_fusion.4
  908.2 260.8 %all-reduce.12.cloned.1.call-done = (f32[1,768,2304]{1,2,0:T(8,128)}, f32[1,768,2304]{1,2,0:T(8,128)}, f32[1,768,768]{2,1,0:T(8,128)}, f32[1,768,768]{2,1,0:T(8,128)}) async-done(((f32[1,768,2304]{1,2,0:T(8,128)}, f32[1,768,2304]{1,2,0:T(8,128)}, f32[1,768,768]{2,1,0:T(8,128)}, f32[1,768,768]{2,1,0:T(8,128)}), (f32[1,768,2304]{1,2,0:T(8,128)}, f32[1,768,2304]{1,2,0:T(8,128)}, f32[1,768,768]{2,1,0:T(8,128)}, ...) | async-done | bytes 18874384 | tf_op jit(solution)/shard_map/psum | solution.py:226
  1169.0 11.0 pad_maximum_fusion
  1179.9 15.4 %copy.101 = f32[2,768,2304]{2,1,0:T(8,128)} copy(f32[2,768,2304]{1,2,0:T(8,128)} %pad_maximum_fusion) | data formatting | bytes 28311552
  1195.4 4.2 pad_maximum_fusion.1
  (286 shorter events, 64.2 us)
Async XLA Ops:
  7.2 91.5 %all-gather.5.cloned.1.call-start = ((), (), s32[]{:S(2)}) async-start(), calls=%async_computation.6 | async-start | bytes 3932160 | tf_op jit(solution)/shard_map/all_gather | solution.py:84
  16.7 5.7 copy-start.14
  17.0 5.4 copy-start.32
  17.3 7.0 copy-start.10
  22.3 4.5 copy-start
  24.3 4.7 copy-start.42
  29.9 146.2 %copy-start.2 = (f32[512,768]{1,0:T(8,128)}, f32[512,768]{1,0:T(8,128)S(1)}, u32[]{:S(2)}) copy-start(f32[512,768]{1,0:T(8,128)S(1)} %get-tuple-element.112) | copy-start | bytes 4718596
  30.0 146.2 %copy-start.53 = (f32[512]{0:T(512)}, f32[512]{0:T(512)S(1)}, u32[]{:S(2)}) copy-start(f32[512]{0:T(512)S(1)} %broadcast_multiply_fusion.3) | copy-start | bytes 6148
  31.0 145.1 %copy-start.55 = (f32[512]{0:T(512)}, f32[512]{0:T(512)S(1)}, u32[]{:S(2)}) copy-start(f32[512]{0:T(512)S(1)} %fusion.80) | copy-start | bytes 6148
  31.1 145.1 %copy-start.51 = (f32[768]{0:T(1024)}, f32[768]{0:T(1024)S(1)}, u32[]{:S(2)}) copy-start(f32[768]{0:T(1024)S(1)} %get-tuple-element.122) | copy-start | bytes 9220
  32.3 143.8 %reduce-scatter.7.cloned.1.call-start = ((), (), s32[]{:S(2)}) async-start(), calls=%async_computation.7 | async-start | bytes 3932160 | tf_op jit(solution)/shard_map/reduce_scatter | solution.py:87
  106.4 5.0 copy-start.8
  106.4 6.7 copy-start.70
  117.0 148.3 %all-gather.7.cloned.1.call-start = ((), (), s32[]{:S(2)}) async-start(), calls=%async_computation.8 | async-start | bytes 3932160 | tf_op jit(solution)/shard_map/all_gather | solution.py:84
  117.8 81.4 %copy-start.59 = (f32[768]{0:T(1024)}, f32[768]{0:T(1024)S(1)}, u32[]{:S(2)}) copy-start(f32[768]{0:T(1024)S(1)} %get-tuple-element.65) | copy-start | bytes 9220
  185.0 7.6 copy-start.16
  187.6 6.9 copy-start.12
  192.5 4.5 copy-start.1
  201.7 141.1 %reduce-scatter.9.cloned.1.call-start = ((), (), s32[]{:S(2)}) async-start(), calls=%async_computation.9 | async-start | bytes 3932160 | tf_op jit(solution)/shard_map/reduce_scatter | solution.py:87
  273.1 5.0 copy-start.9
  273.1 6.6 copy-start.71
  283.7 129.9 %all-gather.9.cloned.1.call-start = ((), (), s32[]{:S(2)}) async-start(), calls=%async_computation.10 | async-start | bytes 3932160 | tf_op jit(solution)/shard_map/all_gather | solution.py:128
  349.9 145.8 %reduce-scatter.11.cloned.1.call-start = ((), (), s32[]{:S(2)}) async-start(), calls=%async_computation.11 | async-start | bytes 3932160 | tf_op jit(solution)/shard_map/reduce_scatter | solution.py:134
  413.6 16.6 %copy-start.40 = (bf16[96,8,2,768]{3,1,2,0:T(8,128)(2,1)S(1)}, bf16[96,8,2,768]{3,1,2,0:T(8,128)(2,1)}, u32[]{:S(2)}) copy-start(bf16[96,8,2,768]{3,1,2,0:T(8,128)(2,1)} %copy.112) | copy-start | bytes 7077892
  425.6 4.6 copy-start.80
  436.6 163.6 %all-gather.11.cloned.1.call-start = ((), (), s32[]{:S(2)}) async-start(), calls=%async_computation.12 | async-start | bytes 3932160 | tf_op jit(solution)/shard_map/all_gather | solution.py:128
  495.7 3.2 copy-start.7
  495.7 3.2 copy-start.29
  502.1 7.7 copy-start.13
  502.1 16.9 %slice-start.3 = ((s8[12582912]{0:T(1024)(128)(4,1)}), s8[4194304]{0:T(1024)(128)(4,1)S(1)}, s32[]{:S(2)}) async-start(s8[12582912]{0:T(1024)(128)(4,1)} %bitcast.151), calls=%async_computation.21 | async-start | bytes 8388608
  502.1 16.9 %slice-start.4 = ((s8[12582912]{0:T(1024)(128)(4,1)}), s8[4194304]{0:T(1024)(128)(4,1)S(1)}, s32[]{:S(2)}) async-start(s8[12582912]{0:T(1024)(128)(4,1)} %bitcast.151), calls=%async_computation.22 | async-start | bytes 8388608
  509.8 9.2 slice-start.5
  519.0 6.9 copy-start.34
  526.0 3.2 slice-start.6
  529.2 4.6 copy-start.37
  536.6 146.5 %reduce-scatter.13.cloned.1.call-start = ((), (), s32[]{:S(2)}) async-start(), calls=%async_computation.13 | async-start | bytes 3932160 | tf_op jit(solution)/shard_map/reduce_scatter | solution.py:134
  600.3 17.3 %copy-start.39 = (bf16[96,8,2,768]{3,1,2,0:T(8,128)(2,1)S(1)}, bf16[96,8,2,768]{3,1,2,0:T(8,128)(2,1)}, u32[]{:S(2)}) copy-start(bf16[96,8,2,768]{3,1,2,0:T(8,128)(2,1)} %copy.111) | copy-start | bytes 7077892
  612.8 4.8 copy-start.82
  624.0 104.1 %reduce-scatter.17.cloned.1.call-start = ((), (), s32[]{:S(2)}) async-start(), calls=%async_computation.15 | async-start | bytes 1327104 | tf_op jit(solution)/shard_map/reduce_scatter | solution.py:233
  630.6 133.3 %reduce-scatter.15.cloned.1.call-start = ((), (), s32[]{:S(2)}) async-start(), calls=%async_computation.14 | async-start | bytes 1327104 | tf_op jit(solution)/shard_map/reduce_scatter | solution.py:233
  655.5 3.9 copy-start.60
  655.5 198.8 %all-reduce.14.cloned.1.call-start = ((), (), s32[]{:S(2)}) async-start(), calls=%async_computation.17 | async-start | bytes 9437184
  655.8 3.6 copy-start.38
  655.8 3.6 copy-start.47
  655.8 3.6 copy-start.50
  655.8 8.6 slice-start.8
  659.4 5.0 copy-start.69
  659.4 5.0 slice-start.9
  679.7 3.4 copy-start.3
  679.7 3.4 copy-start.52
  679.7 3.4 copy-start.54
  679.7 3.4 copy-start.56
  679.8 6.0 copy-start.58
  679.8 489.2 %all-reduce.12.cloned.1.call-start = ((), (), s32[]{:S(2)}) async-start(), calls=%async_computation.16 | async-start | bytes 37748736 | tf_op jit(solution)/shard_map/psum | solution.py:226
  690.9 11.0 slice-start
  691.0 11.6 slice-start.1
  691.0 13.0 %slice-start.2 = ((s8[12582912]{0:T(1024)(128)(4,1)}), s8[4194304]{0:T(1024)(128)(4,1)S(1)}, s32[]{:S(2)}) async-start(s8[12582912]{0:T(1024)(128)(4,1)} %bitcast.149), calls=%async_computation.20 | async-start | bytes 8388608
  704.0 7.0 copy-start.19
  704.0 7.0 copy-start.26
  715.4 3.2 copy-start.48
  728.0 174.6 %copy-start.20 = (f32[512,768]{1,0:T(8,128)S(1)}, f32[512,768]{1,0:T(8,128)}, u32[]{:S(2)}) copy-start(f32[512,768]{1,0:T(8,128)} %copy-done.18) | copy-start | bytes 4718596
  728.0 174.6 %copy-start.36 = (bf16[12,64,512]{2,1,0:T(8,128)(2,1)S(1)}, bf16[12,64,512]{2,1,0:T(8,128)(2,1)}, u32[]{:S(2)}) copy-start(bf16[12,64,512]{2,1,0:T(8,128)(2,1)} %copy-done.35) | copy-start | bytes 2359300
  728.0 174.6 %copy-start.45 = (bf16[12,64,512]{2,1,0:T(8,128)(2,1)S(1)}, bf16[12,64,512]{2,1,0:T(8,128)(2,1)}, u32[]{:S(2)}) copy-start(bf16[12,64,512]{2,1,0:T(8,128)(2,1)} %copy-done.44) | copy-start | bytes 2359300
  1179.9 15.4 %copy-start.41 = (f32[1,768,768]{2,1,0:T(8,128)S(1)}, f32[1,768,768]{2,1,0:T(8,128)}, u32[]{:S(2)}) copy-start(f32[1,768,768]{2,1,0:T(8,128)} %get-tuple-element.80) | copy-start | bytes 7077892
  (41 other events, 76.3 us)
Sparse Core Ops, SparseCore 0:
  32.4 66.1 all-gather.4
  117.2 58.8 reduce-scatter.6
  201.8 63.5 all-gather.6
  283.8 58.8 reduce-scatter.8
  350.0 63.5 all-gather.8
  436.7 58.8 reduce-scatter.10
  536.7 63.5 all-gather.10
  624.2 58.8 reduce-scatter.12
  686.9 36.8 reduce-scatter.16
  727.2 36.7 reduce-scatter.14
  767.3 86.9 all-reduce.13
  862.3 306.5 all-reduce.11
where the time goes:
time: 1220 us; the launch traced here: 1210 us
  waiting for transfers between devices  809 us (66%)
  matrix products  182 us (15%)
  local copies, waits for them, and re-layouts  85.4 us (7%)
  other arithmetic  69 us (6%)
  blocking collectives  41.8 us (3%)
  between operations  17.3 us (1%)
    psum x1, waiting for transfers between devices, shards(): lax.psum((d_wqkv, d_wo, d_gain1, d_bias1, d_gain2, d_bias2), ('dp', 'tens...  261 us
    all_gather x2, waiting for transfers between devices, backward_layer(): lax.all_gather(d_pre2.astype(jnp.bfloat16), 'tensor', axis=0, tiled=True)  127 us
    reduce_scatter x2, waiting for transfers between devices, forward_layer(): lax.psum_scatter(jnp.dot(act_low, wdown, preferred_element_type=jnp.float...  117 us
    all_gather x2, waiting for transfers between devices, forward_layer(): gathered = lax.all_gather(normed_low, 'tensor', axis=0, tiled=True)  117 us
    unnamed x13, waiting for transfers between devices  88.7 us
    reduce_scatter x2, waiting for transfers between devices, backward_layer(): lax.psum_scatter(jnp.dot(d_joined, up_flat.T, preferred_element_type=jnp....  62.3 us
    unnamed x190, local copies, waits for them, and re-layouts  56 us
    psum x1, blocking collectives, shards(): lax.psum((d_wqkv, d_wo, d_gain1, d_bias1, d_gain2, d_bias2), ('dp', 'tens...  41.8 us
  transfers between devices with their start and end apart: 12, of which 11 were waited for; matrix products, arithmetic and copies ran while one was open for 10% of the time, Pallas kernels for 0%

commit v1 on v0

--- a/solution.py
+++ b/solution.py
@@ -10,6 +10,27 @@
 eps_norm = 1e-05
 gelu_coef = 0.7978845608028654
 masked_score = -1e30
+
+
+def gather_around(shard, axis, dim):
+    size, position, rows = (lax.axis_size(axis), lax.axis_index(axis), shard.shape[dim])
+    forward = [(i, (i + 1) % size) for i in range(size)]
+    left = [(i, (i - 1) % size) for i in range(size)]
+    result = jnp.zeros((*shard.shape[:dim], size * rows, *shard.shape[dim + 1 :]), shard.dtype)
+    result = lax.dynamic_update_slice_in_dim(result, shard, position * rows, axis=dim)
+    from_left = from_right = shard
+    halfway = size // 2
+    for turn in range(1, halfway + 1):
+        from_left = lax.ppermute(from_left, axis, forward)
+        result = lax.dynamic_update_slice_in_dim(
+            result, from_left, (position - turn) % size * rows, axis=dim
+        )
+        if turn < size - halfway:
+            from_right = lax.ppermute(from_right, axis, left)
+            result = lax.dynamic_update_slice_in_dim(
+                result, from_right, (position + turn) % size * rows, axis=dim
+            )
+    return result
 
 
 def segments(bucket_one, lens, rows_dev, short_len):
@@ -125,7 +146,7 @@
     up_flat = wup.reshape(width, -1)
     second_pull = jax.vjp(layer_norm, pre_second, g2, b2)[1]
     d_pre2, d_gain2, d_bias2 = second_pull(grad_out)
-    grad_rows = lax.all_gather(d_pre2.astype(jnp.bfloat16), "tensor", axis=0, tiled=True)
+    grad_rows = gather_around(d_pre2.astype(jnp.bfloat16), "tensor", 0)
     d_act = jnp.dot(grad_rows, wdown.T, preferred_element_type=jnp.float32)
     d_down = jnp.dot(act_low.T, grad_rows, preferred_element_type=jnp.float32)
     geglu_pull = jax.vjp(geglu, joined)[1]

time: 1220 us -> 1200 us (0.984)
  waiting for transfers between devices: 809 us -> 751 us
  starting transfers between devices: 1.89 us -> 37.5 us
    all_gather x2 -> x0, waiting for transfers between devices: 127 us -> none  [backward_layer(): lax.all_gather(d_pre2.astype(jnp.bfloat16), 'tensor', axis=0, tiled=True)]
    ppermute x0 -> x6, waiting for transfers between devices: none -> 69.3 us  [the longest x4 67.8 us: gather_around(): from_left = lax.ppermute(from_left, axis, forward)]
    ppermute x0 -> x6, starting transfers between devices: none -> 35.9 us  [the longest x4 30.2 us: gather_around(): from_left = lax.ppermute(from_left, axis, forward)]
    unnamed x190 -> x196, local copies, waits for them, and re-layouts: 56 us -> 51.6 us
    unnamed x13 -> x11, waiting for transfers between devices: 88.7 us -> 88.7 us
  transfers between devices with their start and end apart: 12 -> 16, of which waited for: 11 -> 14; matrix products, arithmetic and copies ran while one was open for 10% -> 11% of each run, Pallas kernels for 0% -> 0%
where the time goes in v1:
time: 1200 us; the launch traced here: 1190 us
  waiting for transfers between devices  751 us (63%)
  matrix products  185 us (15%)
  local copies, waits for them, and re-layouts  87.9 us (7%)
  other arithmetic  69.6 us (6%)
  blocking collectives  41.8 us (3%)
  starting transfers between devices  37.5 us (3%)
  between operations  17.3 us (1%)
    psum x1, waiting for transfers between devices, shards(): lax.psum((d_wqkv, d_wo, d_gain1, d_bias1, d_gain2, d_bias2), ('dp', 'tens...  261 us
    reduce_scatter x2, waiting for transfers between devices, forward_layer(): lax.psum_scatter(jnp.dot(act_low, wdown, preferred_element_type=jnp.float...  117 us
    all_gather x2, waiting for transfers between devices, forward_layer(): gathered = lax.all_gather(normed_low, 'tensor', axis=0, tiled=True)  117 us
    unnamed x11, waiting for transfers between devices  88.7 us
    ppermute x4, waiting for transfers between devices, gather_around(): from_left = lax.ppermute(from_left, axis, forward)  67.8 us
    reduce_scatter x2, waiting for transfers between devices, backward_layer(): lax.psum_scatter(jnp.dot(d_joined, up_flat.T, preferred_element_type=jnp....  62.7 us
    unnamed x196, local copies, waits for them, and re-layouts  51.6 us
    psum x1, blocking collectives, shards(): lax.psum((d_wqkv, d_wo, d_gain1, d_bias1, d_gain2, d_bias2), ('dp', 'tens...  41.8 us
  transfers between devices with their start and end apart: 16, of which 14 were waited for; matrix products, arithmetic and copies ran while one was open for 11% of the time, Pallas kernels for 0%

profile of v1, /device:TPU:0, one launch (start us, length us, event | category | flops | bytes accessed | tf_op | source)
XLA Modules:
  0.0 1190.1 jit_solution(2637360374122648278)
XLA Ops:
  12.0 4.2 convolution_convert_fusion.1
  17.3 5.0 fusion.103
  24.3 2.6 copy-done
  32.6 7.0 fusion.100
  41.5 57.2 %all-gather.3.cloned.1.call-done = bf16[2048,768]{1,0:T(8,128)(2,1)} async-done(((bf16[512,768]{1,0:T(8,128)(2,1)}), bf16[2048,768]{1,0:T(8,128)(2,1)}) %all-gather.3.cloned.1.call-update) | async-done | bytes 3145744 | tf_op jit(solution)/shard_map/all_gather | solution.py:105
  98.7 7.7 fusion.107
  106.5 2.2 multiply_convert_fusion.3
  108.7 2.8 copy-done.8
  113.2 3.9 convolution_convert_fusion.5
  117.9 58.3 %reduce-scatter.7.cloned.1.call-done = bf16[512,768]{1,0:T(8,128)(2,1)} async-done(((bf16[2048,768]{1,0:T(8,128)(2,1)}), bf16[512,768]{1,0:T(8,128)(2,1)}) %reduce-scatter.7.cloned.1.call-update) | async-done | bytes 786448 | tf_op jit(solution)/shard_map/reduce_scatter | solution.py:108
  178.2 4.1 convolution_convert_fusion
  187.7 5.0 fusion.105
  194.6 2.6 copy-done.1
  197.2 2.1 fusion.48
  202.0 3.5 copy.112
  205.5 59.9 %all-gather.5.cloned.1.call-done = bf16[2048,768]{1,0:T(8,128)(2,1)} async-done(((bf16[512,768]{1,0:T(8,128)(2,1)}), bf16[2048,768]{1,0:T(8,128)(2,1)}) %all-gather.5.cloned.1.call-update) | async-done | bytes 3145744 | tf_op jit(solution)/shard_map/all_gather | solution.py:105
  265.5 7.7 fusion.108
  273.3 2.2 multiply_convert_fusion.2
  275.5 2.8 copy-done.9
  279.9 3.9 convolution_convert_fusion.4
  283.9 59.0 %reduce-scatter.9.cloned.1.call-done = bf16[512,768]{1,0:T(8,128)(2,1)} async-done(((bf16[2048,768]{1,0:T(8,128)(2,1)}), bf16[512,768]{1,0:T(8,128)(2,1)}) %reduce-scatter.9.cloned.1.call-update) | async-done | bytes 786448 | tf_op jit(solution)/shard_map/reduce_scatter | solution.py:108
  351.9 2.8 collective-permute-start.1
  354.8 18.8 %collective-permute-done = bf16[512,768]{1,0:T(8,128)(2,1)} collective-permute-done((bf16[512,768]{1,0:T(8,128)(2,1)}, bf16[512,768]{1,0:T(8,128)(2,1)}, u32[]{:S(2)}, u32[]{:S(2)}) %collective-permute-start) | collective-permute-done | bytes 786464 | tf_op jit(solution)/shard_map/ppermute | solution.py:24
  373.6 14.2 %collective-permute-start.2 = (bf16[512,768]{1,0:T(8,128)(2,1)}, bf16[512,768]{1,0:T(8,128)(2,1)}, u32[]{:S(2)}, u32[]{:S(2)}) collective-permute-start(bf16[512,768]{1,0:T(8,128)(2,1)} %collective-permute-done), channel_id=1, source_target_pairs={{0,1},{1,2},{2,3},{3,0},{4,5},{5,6},{6,7},{7,4},{8,9},{9,10},{10,1... | collective-permute-start | bytes 2359304 | tf_op jit(solution)/shard_map/ppermute | solution.py:24
  387.8 2.2 constant_dynamic-update-slice_fusion.5
  392.1 13.8 %collective-permute-done.2 = bf16[512,768]{1,0:T(8,128)(2,1)} collective-permute-done((bf16[512,768]{1,0:T(8,128)(2,1)}, bf16[512,768]{1,0:T(8,128)(2,1)}, u32[]{:S(2)}, u32[]{:S(2)}) %collective-permute-start.2) | collective-permute-done | bytes 786464 | tf_op jit(solution)/shard_map/ppermute | solution.py:24
  408.0 12.6 %fusion.25 = (f32[2048,768]{1,0:T(8,128)S(1)}, f32[2048,768]{1,0:T(8,128)S(1)}) fusion(f32[2048,1536]{1,0:T(8,128)} %copy-done.9, bf16[2048,768]{1,0:T(8,128)(2,1)} %constant_dynamic-update-slice_fusion.3, bf16[2,768,768]{2,1,0:T(8,128)(2,1)S(1)} %copy-done.73), kind=kOutput, calls=%fused_computation.70 | convolution fusion | flops 2456813568 | bytes 29491200 | tf_op jit(solution)/shard_map/dot_general | solution.py:150
  420.6 2.6 copy-done.81
  425.1 6.4 convolution_convert_fusion.7
  431.7 59.2 %reduce-scatter.11.cloned.1.call-done = bf16[512,768]{1,0:T(8,128)(2,1)} async-done(((bf16[2048,768]{1,0:T(8,128)(2,1)}), bf16[512,768]{1,0:T(8,128)(2,1)}) %reduce-scatter.11.cloned.1.call-update) | async-done | bytes 786448 | tf_op jit(solution)/shard_map/reduce_scatter | solution.py:155
  490.9 3.2 multiply_reduce_fusion.3
  497.3 7.7 fusion.51
  505.0 9.4 multiply_reduce_fusion.1
  514.4 6.9 multiply_convert_fusion.1
  526.5 2.6 multiply_reduce_fusion.2
  531.9 2.8 collective-permute-start.4
  534.7 18.5 %collective-permute-done.3 = bf16[512,768]{1,0:T(8,128)(2,1)S(1)} collective-permute-done((bf16[512,768]{1,0:T(8,128)(2,1)S(1)}, bf16[512,768]{1,0:T(8,128)(2,1)S(1)}, u32[]{:S(2)}, u32[]{:S(2)}) %collective-permute-start.3) | collective-permute-done | bytes 786464 | tf_op jit(solution)/shard_map/ppermute | solution.py:24
  553.2 14.0 %collective-permute-start.5 = (bf16[512,768]{1,0:T(8,128)(2,1)S(1)}, bf16[512,768]{1,0:T(8,128)(2,1)S(1)}, u32[]{:S(2)}, u32[]{:S(2)}) collective-permute-start(bf16[512,768]{1,0:T(8,128)(2,1)S(1)} %collective-permute-done.3), channel_id=1, source_target_pairs={{0,1},{1,2},{2,3},{3,0},{4,5},{5,6},{6,7},{7,4},{8,9},{9,10},{10,1... | collective-permute-start | bytes 2359304 | tf_op jit(solution)/shard_map/ppermute | solution.py:24
  568.8 16.7 %collective-permute-done.5 = bf16[512,768]{1,0:T(8,128)(2,1)S(1)} collective-permute-done((bf16[512,768]{1,0:T(8,128)(2,1)S(1)}, bf16[512,768]{1,0:T(8,128)(2,1)S(1)}, u32[]{:S(2)}, u32[]{:S(2)}) %collective-permute-start.5) | collective-permute-done | bytes 786464 | tf_op jit(solution)/shard_map/ppermute | solution.py:24
  585.7 11.9 %fusion.24 = (f32[2048,768]{1,0:T(8,128)}, f32[2048,768]{1,0:T(8,128)}) fusion(f32[2048,1536]{1,0:T(8,128)S(1)} %bitcast.154, bf16[2048,768]{1,0:T(8,128)(2,1)S(1)} %constant_dynamic-update-slice_fusion.7, bf16[2,768,768]{2,1,0:T(8,128)(2,1)} %param.20), kind=kOutput, calls=%fused_computation.69 | convolution fusion | flops 2456813568 | bytes 29491200 | tf_op jit(solution)/shard_map/dot_general | solution.py:150
  597.6 9.3 convolution_convert_fusion.6
  607.2 6.5 convolution_convert_fusion.8
  613.8 12.0 %convolution_convert_fusion.2 = bf16[768,1536]{1,0:T(8,128)(2,1)} fusion(bf16[2048,768]{1,0:T(8,128)(2,1)} %all-gather.5.cloned.1.call-done, f32[2048,768]{1,0:T(8,128)} %copy-done.82, f32[2048,768]{1,0:T(8,128)} %copy-done.81), kind=kOutput, calls=%fused_computation.50 | convolution fusion | flops 4839309312 | bytes 18087936 | tf_op jit(solution)/shard_map/dot_general | solution.py:154
  625.8 6.0 convert_element_type.181
  631.8 6.6 convolution_convert_fusion.9
  638.7 3.6 convolution_bitcast_fusion.2
  642.3 5.0 convolution_bitcast_fusion
  647.4 9.3 convolution_convert_fusion.3
  656.7 6.0 convert_element_type.179
  662.7 3.5 reduce-scatter.13.cloned.1.call-done
  666.3 2.6 multiply_reduce_fusion.4
  674.1 10.9 multiply_reduce_fusion
  687.2 7.0 multiply_convert_fusion
  694.2 2.3 convolution_bitcast_fusion.3
  702.7 5.0 convolution_bitcast_fusion.1
  709.9 2.6 pad_maximum_fusion.4
  712.6 34.7 %reduce-scatter.15.cloned.1.call-done = bf16[768,96]{0,1:T(8,128)(2,1)} async-done(((bf16[768,768]{0,1:T(8,128)(2,1)}), bf16[768,96]{0,1:T(8,128)(2,1)}) %reduce-scatter.15.cloned.1.call-update) | async-done | bytes 147472 | tf_op jit(solution)/shard_map/reduce_scatter | solution.py:254
  749.1 88.5 %all-reduce.14.cloned.1.call-done = (bf16[768,2,768]{2,1,0:T(2,128)(2,1)}, bf16[768,2,768]{2,1,0:T(2,128)(2,1)}) async-done(((bf16[768,2,768]{2,1,0:T(2,128)(2,1)}, bf16[768,2,768]{2,1,0:T(2,128)(2,1)}), (bf16[768,2,768]{2,1,0:T(2,128)(2,1)}, bf16[768,2,768]{2,1,0:T(2,128)(2,1)})) %all-reduce.14.cloned.1.call-update) | async-done | bytes 4718608
  841.7 41.8 %all-reduce.6 = (f32[1,768]{1,0:T(1,128)S(1)}, f32[1,768]{1,0:T(1,128)S(1)}, f32[1,768]{1,0:T(1,128)S(1)}, f32[1,768]{1,0:T(1,128)S(1)}, f32[1,768]{1,0:T(1,128)...) all-reduce(f32[1,768]{1,0:T(1,128)S(1)} %stack.101, ...), channel_id=1, replica_groups=mesh['dp'=8,'tensor'=4] {'dp','tensor'}, use_global_device_ids=true, to_apply=%region_35.36 | all-reduce | flops 6144 | bytes 49152 | tf_op jit(solution)/shard_map/psum | solution.py:247
  885.9 5.5 add_add_fusion.4
  891.4 260.8 %all-reduce.12.cloned.1.call-done = (f32[1,768,2304]{1,2,0:T(8,128)}, f32[1,768,2304]{1,2,0:T(8,128)}, f32[1,768,768]{2,1,0:T(8,128)}, f32[1,768,768]{2,1,0:T(8,128)}) async-done(((f32[1,768,2304]{1,2,0:T(8,128)}, f32[1,768,2304]{1,2,0:T(8,128)}, f32[1,768,768]{2,1,0:T(8,128)}, f32[1,768,768]{2,1,0:T(8,128)}), (f32[1,768,2304]{1,2,0:T(8,128)}, f32[1,768,2304]{1,2,0:T(8,128)}, f32[1,768,768]{2,1,0:T(8,128)}, ...) | async-done | bytes 18874384 | tf_op jit(solution)/shard_map/psum | solution.py:247
  1152.2 11.0 pad_maximum_fusion
  1163.2 15.4 %copy.101 = f32[2,768,2304]{2,1,0:T(8,128)} copy(f32[2,768,2304]{1,2,0:T(8,128)} %pad_maximum_fusion) | data formatting | bytes 28311552
  1178.6 4.2 pad_maximum_fusion.1
  (307 shorter events, 82.3 us)
Async XLA Ops:
  7.2 91.5 %all-gather.3.cloned.1.call-start = ((), (), s32[]{:S(2)}) async-start(), calls=%async_computation.6 | async-start | bytes 3932160 | tf_op jit(solution)/shard_map/all_gather | solution.py:105
  16.7 5.7 copy-start.14
  17.0 5.4 copy-start.33
  17.3 7.0 copy-start.10
  22.3 4.6 copy-start
  24.3 4.7 copy-start.43
  30.0 146.3 %copy-start.2 = (f32[512,768]{1,0:T(8,128)}, f32[512,768]{1,0:T(8,128)S(1)}, u32[]{:S(2)}) copy-start(f32[512,768]{1,0:T(8,128)S(1)} %get-tuple-element.116) | copy-start | bytes 4718596
  30.0 146.2 %copy-start.54 = (f32[512]{0:T(512)}, f32[512]{0:T(512)S(1)}, u32[]{:S(2)}) copy-start(f32[512]{0:T(512)S(1)} %broadcast_multiply_fusion.3) | copy-start | bytes 6148
  31.1 145.1 %copy-start.56 = (f32[512]{0:T(512)}, f32[512]{0:T(512)S(1)}, u32[]{:S(2)}) copy-start(f32[512]{0:T(512)S(1)} %fusion.80) | copy-start | bytes 6148
  31.1 145.1 %copy-start.52 = (f32[768]{0:T(1024)}, f32[768]{0:T(1024)S(1)}, u32[]{:S(2)}) copy-start(f32[768]{0:T(1024)S(1)} %get-tuple-element.126) | copy-start | bytes 9220
  32.4 143.9 %reduce-scatter.7.cloned.1.call-start = ((), (), s32[]{:S(2)}) async-start(), calls=%async_computation.7 | async-start | bytes 3932160 | tf_op jit(solution)/shard_map/reduce_scatter | solution.py:108
  106.5 5.0 copy-start.8
  106.5 6.7 copy-start.71
  117.2 148.3 %all-gather.5.cloned.1.call-start = ((), (), s32[]{:S(2)}) async-start(), calls=%async_computation.8 | async-start | bytes 3932160 | tf_op jit(solution)/shard_map/all_gather | solution.py:105
  117.9 81.4 %copy-start.60 = (f32[768]{0:T(1024)}, f32[768]{0:T(1024)S(1)}, u32[]{:S(2)}) copy-start(f32[768]{0:T(1024)S(1)} %get-tuple-element.65) | copy-start | bytes 9220
  185.1 7.6 copy-start.16
  187.7 6.9 copy-start.12
  192.7 4.5 copy-start.1
  201.8 141.1 %reduce-scatter.9.cloned.1.call-start = ((), (), s32[]{:S(2)}) async-start(), calls=%async_computation.9 | async-start | bytes 3932160 | tf_op jit(solution)/shard_map/reduce_scatter | solution.py:108
  273.2 5.0 copy-start.9
  273.3 6.7 copy-start.72
  283.9 207.0 %reduce-scatter.11.cloned.1.call-start = ((), (), s32[]{:S(2)}) async-start(), calls=%async_computation.10 | async-start | bytes 3932160 | tf_op jit(solution)/shard_map/reduce_scatter | solution.py:155
  351.0 22.6 %collective-permute-start = (bf16[512,768]{1,0:T(8,128)(2,1)}, bf16[512,768]{1,0:T(8,128)(2,1)}, u32[]{:S(2)}, u32[]{:S(2)}) collective-permute-start(bf16[512,768]{1,0:T(8,128)(2,1)} %get-tuple-element.93), channel_id=1, source_target_pairs={{0,1},{1,2},{2,3},{3,0},{4,5},{5,6},{6,7},{7,4},{8,9},{9,10},{10,1... | collective-permute-start | bytes 2359304 | tf_op jit(solution)/shard_map/ppermute | solution.py:24
  351.9 38.1 %collective-permute-start.1 = (bf16[512,768]{1,0:T(8,128)(2,1)}, bf16[512,768]{1,0:T(8,128)(2,1)}, u32[]{:S(2)}, u32[]{:S(2)}) collective-permute-start(bf16[512,768]{1,0:T(8,128)(2,1)} %get-tuple-element.93), channel_id=1, source_target_pairs={{0,3},{1,0},{2,1},{3,2},{4,7},{5,4},{6,5},{7,6},{8,11},{9,8},{10,9... | collective-permute-start | bytes 2359304 | tf_op jit(solution)/shard_map/ppermute | solution.py:29
  373.6 32.3 %collective-permute-start.2 = (bf16[512,768]{1,0:T(8,128)(2,1)}, bf16[512,768]{1,0:T(8,128)(2,1)}, u32[]{:S(2)}, u32[]{:S(2)}) collective-permute-start(bf16[512,768]{1,0:T(8,128)(2,1)} %collective-permute-done), channel_id=1, source_target_pairs={{0,1},{1,2},{2,3},{3,0},{4,5},{5,6},{6,7},{7,4},{8,9},{9,10},{10,1... | collective-permute-start | bytes 2359304 | tf_op jit(solution)/shard_map/ppermute | solution.py:24
  387.8 20.2 %copy-start.73 = (bf16[2,768,768]{2,1,0:T(8,128)(2,1)S(1)}, bf16[2,768,768]{2,1,0:T(8,128)(2,1)}, u32[]{:S(2)}) copy-start(bf16[2,768,768]{2,1,0:T(8,128)(2,1)} %param.20) | copy-start | bytes 7077892
  408.0 17.2 %copy-start.41 = (bf16[96,8,2,768]{3,1,2,0:T(8,128)(2,1)S(1)}, bf16[96,8,2,768]{3,1,2,0:T(8,128)(2,1)}, u32[]{:S(2)}) copy-start(bf16[96,8,2,768]{3,1,2,0:T(8,128)(2,1)} %copy.112) | copy-start | bytes 7077892
  420.6 4.6 copy-start.82
  431.6 234.6 %reduce-scatter.13.cloned.1.call-start = ((), (), s32[]{:S(2)}) async-start(), calls=%async_computation.11 | async-start | bytes 3932160 | tf_op jit(solution)/shard_map/reduce_scatter | solution.py:155
  497.3 7.7 copy-start.13
  497.3 17.1 %slice-start.3 = ((s8[12582912]{0:T(1024)(128)(4,1)}), s8[4194304]{0:T(1024)(128)(4,1)S(1)}, s32[]{:S(2)}) async-start(s8[12582912]{0:T(1024)(128)(4,1)} %bitcast.151), calls=%async_computation.19 | async-start | bytes 8388608
  497.3 17.1 %slice-start.4 = ((s8[12582912]{0:T(1024)(128)(4,1)}), s8[4194304]{0:T(1024)(128)(4,1)S(1)}, s32[]{:S(2)}) async-start(s8[12582912]{0:T(1024)(128)(4,1)} %bitcast.151), calls=%async_computation.20 | async-start | bytes 8388608
  505.0 9.4 slice-start.5
  514.4 6.9 copy-start.35
  524.5 4.6 copy-start.38
  526.5 59.1 %slice-start.6 = ((s8[12582912]{0:T(1024)(128)(4,1)}), s8[4194304]{0:T(1024)(128)(4,1)S(1)}, s32[]{:S(2)}) async-start(s8[12582912]{0:T(1024)(128)(4,1)} %bitcast.153), calls=%async_computation.22 | async-start | bytes 8388608
  526.5 59.1 %slice-start.7 = ((s8[12582912]{0:T(1024)(128)(4,1)}), s8[4194304]{0:T(1024)(128)(4,1)S(1)}, s32[]{:S(2)}) async-start(s8[12582912]{0:T(1024)(128)(4,1)} %bitcast.153), calls=%async_computation.23 | async-start | bytes 8388608
  529.1 56.5 %slice-start.8 = ((s8[12582912]{0:T(1024)(128)(4,1)}), s8[4194304]{0:T(1024)(128)(4,1)S(1)}, s32[]{:S(2)}) async-start(s8[12582912]{0:T(1024)(128)(4,1)} %bitcast.153), calls=%async_computation.24 | async-start | bytes 8388608
  530.9 22.3 %collective-permute-start.3 = (bf16[512,768]{1,0:T(8,128)(2,1)S(1)}, bf16[512,768]{1,0:T(8,128)(2,1)S(1)}, u32[]{:S(2)}, u32[]{:S(2)}) collective-permute-start(bf16[512,768]{1,0:T(8,128)(2,1)S(1)} %get-tuple-element.87), channel_id=1, source_target_pairs={{0,1},{1,2},{2,3},{3,0},{4,5},{5,6},{6,7},{7,4},{8,9},{9,10},{10,1... | collective-permute-start | bytes 2359304 | tf_op jit(solution)/shard_map/ppermute | solution.py:24
  531.9 36.9 %collective-permute-start.4 = (bf16[512,768]{1,0:T(8,128)(2,1)S(1)}, bf16[512,768]{1,0:T(8,128)(2,1)S(1)}, u32[]{:S(2)}, u32[]{:S(2)}) collective-permute-start(bf16[512,768]{1,0:T(8,128)(2,1)S(1)} %get-tuple-element.87), channel_id=1, source_target_pairs={{0,3},{1,0},{2,1},{3,2},{4,7},{5,4},{6,5},{7,6},{8,11},{9,8},{10,9... | collective-permute-start | bytes 2359304 | tf_op jit(solution)/shard_map/ppermute | solution.py:29
  553.2 32.4 %collective-permute-start.5 = (bf16[512,768]{1,0:T(8,128)(2,1)S(1)}, bf16[512,768]{1,0:T(8,128)(2,1)S(1)}, u32[]{:S(2)}, u32[]{:S(2)}) collective-permute-start(bf16[512,768]{1,0:T(8,128)(2,1)S(1)} %collective-permute-done.3), channel_id=1, source_target_pairs={{0,1},{1,2},{2,3},{3,0},{4,5},{5,6},{6,7},{7,4},{8,9},{9,10},{10,1... | collective-permute-start | bytes 2359304 | tf_op jit(solution)/shard_map/ppermute | solution.py:24
  585.7 12.0 %copy-start.24 = (bf16[2048,768]{1,0:T(8,128)(2,1)}, bf16[2048,768]{1,0:T(8,128)(2,1)S(1)}, u32[]{:S(2)}) copy-start(bf16[2048,768]{1,0:T(8,128)(2,1)S(1)} %constant_dynamic-update-slice_fusion.7) | copy-start | bytes 9437188
  585.7 12.0 %copy-start.40 = (bf16[96,8,2,768]{3,1,2,0:T(8,128)(2,1)S(1)}, bf16[96,8,2,768]{3,1,2,0:T(8,128)(2,1)}, u32[]{:S(2)}) copy-start(bf16[96,8,2,768]{3,1,2,0:T(8,128)(2,1)} %copy.111) | copy-start | bytes 7077892
  607.0 105.6 %reduce-scatter.17.cloned.1.call-start = ((), (), s32[]{:S(2)}) async-start(), calls=%async_computation.13 | async-start | bytes 1327104 | tf_op jit(solution)/shard_map/reduce_scatter | solution.py:254
  613.7 133.5 %reduce-scatter.15.cloned.1.call-start = ((), (), s32[]{:S(2)}) async-start(), calls=%async_computation.12 | async-start | bytes 1327104 | tf_op jit(solution)/shard_map/reduce_scatter | solution.py:254
  638.4 199.2 %all-reduce.14.cloned.1.call-start = ((), (), s32[]{:S(2)}) async-start(), calls=%async_computation.15 | async-start | bytes 9437184
  638.7 8.7 slice-start.11
  642.3 5.1 copy-start.70
  642.3 5.1 slice-start.12
  662.7 6.2 copy-start.59
  662.7 489.5 %all-reduce.12.cloned.1.call-start = ((), (), s32[]{:S(2)}) async-start(), calls=%async_computation.14 | async-start | bytes 37748736 | tf_op jit(solution)/shard_map/psum | solution.py:247
  669.8 4.3 copy-start.11
  669.8 4.3 copy-start.44
  674.1 11.0 slice-start
  674.1 11.7 slice-start.1
  674.1 13.1 %slice-start.2 = ((s8[12582912]{0:T(1024)(128)(4,1)}), s8[4194304]{0:T(1024)(128)(4,1)S(1)}, s32[]{:S(2)}) async-start(s8[12582912]{0:T(1024)(128)(4,1)} %bitcast.149), calls=%async_computation.18 | async-start | bytes 8388608
  687.2 7.0 copy-start.19
  687.2 7.0 copy-start.27
  707.7 4.8 copy-start.65
  707.7 4.8 copy-start.64
  709.9 176.1 %copy-start.20 = (f32[512,768]{1,0:T(8,128)S(1)}, f32[512,768]{1,0:T(8,128)}, u32[]{:S(2)}) copy-start(f32[512,768]{1,0:T(8,128)} %copy-done.18) | copy-start | bytes 4718596
  709.9 176.1 %copy-start.37 = (bf16[12,64,512]{2,1,0:T(8,128)(2,1)S(1)}, bf16[12,64,512]{2,1,0:T(8,128)(2,1)}, u32[]{:S(2)}) copy-start(bf16[12,64,512]{2,1,0:T(8,128)(2,1)} %copy-done.36) | copy-start | bytes 2359300
  709.9 176.0 %copy-start.48 = (bf16[12,64,512]{2,1,0:T(8,128)(2,1)S(1)}, bf16[12,64,512]{2,1,0:T(8,128)(2,1)}, u32[]{:S(2)}) copy-start(bf16[12,64,512]{2,1,0:T(8,128)(2,1)} %copy-done.47) | copy-start | bytes 2359300
  1163.2 15.4 %copy-start.42 = (f32[1,768,768]{2,1,0:T(8,128)S(1)}, f32[1,768,768]{2,1,0:T(8,128)}, u32[]{:S(2)}) copy-start(f32[1,768,768]{2,1,0:T(8,128)} %get-tuple-element.80) | copy-start | bytes 7077892
  (48 other events, 106.8 us)
Sparse Core Ops, SparseCore 0:
  32.5 66.1 all-gather.2
  117.3 58.8 reduce-scatter.6
  201.9 63.5 all-gather.4
  284.0 58.8 reduce-scatter.8
  431.7 59.0 reduce-scatter.10
  607.1 59.1 reduce-scatter.12
  670.0 36.7 reduce-scatter.16
  710.4 36.7 reduce-scatter.14
  750.6 86.9 all-reduce.13
  845.6 306.5 all-reduce.11
